TPU v7x, 512 devices: a whole 4x8x8 slice. The times are simulated.
512 devices in a mesh: blk: 8 (over y_lo, core), team: 64 (over y_hi, x, z).
Axes of the slice: x: 4, y: 8 (y_hi: 2, y_lo: 4; y = y_hi * 4 + y_lo), z: 8, core: 2. Of those that a mesh axis runs over, the one named last changes fastest.
Arguments:
- features: bfloat16 [65536, 256], P(('blk', 'team')), may hold values from -6 to 6
- weight: bfloat16 [256, 256], replicated, may hold values from -0.375 to 0.375
- bias: float32 [256], replicated, may hold values from -3 to 3
- cotangent: bfloat16 [65536, 256], P(('blk', 'team')), may hold values from -6 to 6
- adj_cols: int32 [64, 8, 8, 12], P('team', None, 'blk'), may hold values from 0 to 63, as said below
- adj_vals: bfloat16 [64, 8, 8, 12, 128, 128], P('team', None, 'blk'), as said below
Outputs:
- hidden: bfloat16 [65536, 256], P(('blk', 'team'))
- grad_input: bfloat16 [65536, 256], P(('blk', 'team'))
- grad_weight: float32 [256, 256], replicated
- grad_bias: float32 [256], replicated
Inputs may be any that keep to these rules, and one draw needn't show every extreme that they name: `adj_cols`: for every node panel and column group the 12 entries are distinct. Block (i, j) of A is listed exactly when block (j, i) is, every column panel is listed by exactly 12 row panels of each column group, and A is symmetric. `adj_vals`: the block listed for panels (i, j) is the transpose of the block listed for (j, i), so A is symmetric.
All inputs are finite; a program needn't handle non-finite values.
Results may differ from a plain program's by a relative error of at most 0.0075.
Values may be sent and summed in bfloat16 or wider, within the bound.
No kernel may reach another device: no remote copies, remote signals or barrier semaphores. Data moves between devices by JAX's collectives and lax.ppermute only.
A program may use at most 64 MiB of HBM per device.

v0:
```python
import jax
import jax.numpy as jnp
from jax import lax
from jax.sharding import Mesh
from jax.sharding import PartitionSpec as P

BLK_AXES = ("y_lo", "core")
TEAM_AXES = ("y_hi", "x", "z")
PLANE = ("x", "z")
ALL_AXES = BLK_AXES + TEAM_AXES


def fine_mesh(mesh):
    blk = mesh.shape["blk"]
    team = mesh.shape["team"]
    sizes = (blk // 2, 2, 2, 4, team // 8)
    return Mesh(mesh.devices.reshape(sizes), ALL_AXES)


def gather_team(rows):
    other = lax.ppermute(rows, "y_hi", perm=[(0, 1), (1, 0)])
    pair = jnp.stack([rows, other], axis=0)
    full = lax.all_gather(pair, PLANE, axis=0, tiled=True)
    return full.reshape(-1, rows.shape[1])


def member_slots(members, plane_size):
    my_hi = lax.axis_index("y_hi")
    return members % plane_size * 2 + (members // plane_size != my_hi).astype(jnp.int32)


def collect(panels, slots, adj_vals):
    block = adj_vals.shape[-1]
    width = panels.shape[1]
    stacked = panels.reshape(panels.shape[0] // block, block, width)
    picked = jnp.take(stacked, slots, axis=0)
    summed = jnp.einsum(
        "rkij,rkjf->rif", adj_vals[0, :, 0], picked, preferred_element_type=jnp.float32
    )
    return summed.reshape(-1, width)


def activation(value):
    return jax.nn.gelu(value, approximate=True)


def local(features, weight, bias, cotangent, adj_cols, adj_vals):
    plane_size = lax.psum(1, PLANE)
    slots = member_slots(adj_cols[0, :, 0, :], plane_size)
    product = jnp.dot(features, weight, preferred_element_type=jnp.float32).astype(jnp.bfloat16)
    gathered = gather_team(product)
    partial_rows = collect(gathered, slots, adj_vals)
    summed = lax.psum_scatter(partial_rows, BLK_AXES, scatter_dimension=0, tiled=True)
    pre = summed + bias[None, :]
    activated, pullback = jax.vjp(activation, pre)
    hidden = activated.astype(jnp.bfloat16)
    pulled = pullback(cotangent.astype(jnp.float32))[0].astype(jnp.bfloat16)
    pulled_group = gather_team(pulled)
    partial_back = collect(pulled_group, slots, adj_vals)
    spread = lax.psum_scatter(partial_back, BLK_AXES, scatter_dimension=0, tiled=True).astype(
        jnp.bfloat16
    )
    grad_input = jnp.dot(spread, weight.T, preferred_element_type=jnp.float32).astype(jnp.bfloat16)
    local_weight = lax.dot_general(
        features, spread, (((0,), (0,)), ((), ())), preferred_element_type=jnp.float32
    )
    local_bias = jnp.sum(pulled.astype(jnp.float32), axis=0)
    both = jnp.concatenate([local_weight, local_bias[None, :]], axis=0)
    both = lax.psum(both, PLANE)
    both = lax.psum(both, ("y_lo", "y_hi", "core"))
    grad_weight = both[:-1]
    grad_bias = both[-1]
    return (hidden, grad_input, grad_weight, grad_bias)


def solution(mesh):
    fine = fine_mesh(mesh)
    rows = P(ALL_AXES, None)
    return jax.shard_map(
        local,
        mesh=fine,
        in_specs=(
            rows,
            P(),
            P(),
            rows,
            P(TEAM_AXES, None, BLK_AXES, None),
            P(TEAM_AXES, None, BLK_AXES, None, None, None),
        ),
        out_specs=(rows, rows, P(), P()),
        check_vma=False,
    )
```

profile of v0, /device:TPU:1, one launch (start us, length us, event | category | flops | bytes accessed | tf_op | source)
XLA Modules:
  0.0 590.6 jit_solution(9726838023997011577)
XLA Ops:
  7.2 0.0 copy-start
  7.2 0.0 all-gather.3.cloned.1.call-start
  7.2 1.2 convolution_convert_fusion.1
  8.5 8.3 %collective-permute-start = (bf16[128,256]{1,0:T(8,128)(2,1)S(1)}, bf16[128,256]{1,0:T(8,128)(2,1)S(1)}, u32[]{:S(2)}, u32[]{:S(2)}) collective-permute-start(bf16[128,256]{1,0:T(8,128)(2,1)S(1)} %convolution_convert_fusion.1), channel_id=1, source_target_pairs={{0,32},{32,0},{1,33},{33,1},{2,34},{34,2},{3,35},{35,3},{4,36},{36... | collective-permute-start | bytes 196616 | tf_op jit(solution)/shard_map/ppermute | solution.py:21
  16.8 1.7 collective-permute-done
  18.5 0.7 pad_maximum_fusion.1
  19.1 0.0 all-gather.3.cloned.1.call-update
  19.2 0.0 reduce-scatter.3.cloned.1.call-start
  19.2 0.7 compare_and_fusion
  19.9 0.1 reshape.42
  20.0 91.1 %all-gather.3.cloned.1.call-done = bf16[64,128,256]{2,1,0:T(8,128)(2,1)} async-done(((bf16[2,128,256]{2,1,0:T(8,128)(2,1)}), bf16[64,128,256]{2,1,0:T(8,128)(2,1)}) %all-gather.3.cloned.1.call-update) | async-done | bytes 4194320 | tf_op jit(solution)/shard_map/all_gather | solution.py:23
  111.1 8.2 %gather_fusion = bf16[96,128,256]{2,1,0:T(8,128)(2,1)} fusion(bf16[64,128,256]{2,1,0:T(8,128)(2,1)} %all-gather.3.cloned.1.call-done, s32[1024]{0:T(1024)S(1)} %pad_clamp_fusion), kind=kCustom, calls=%fused_computation.clone | custom fusion | bytes 12583296 | tf_op jit(solution)/shard_map/jit(_take)/gather | solution.py:36
  119.3 0.0 copy-done
  119.3 0.0 copy-start.3
  119.3 0.0 copy-start.4
  119.3 5.2 fusion.2
  124.5 0.0 reduce-scatter.3.cloned.1.call-update
  124.5 0.0 all-gather.5.cloned.1.call-start
  124.6 38.0 %reduce-scatter.3.cloned.1.call-done = f32[128,256]{1,0:T(8,128)} async-done(((f32[1024,256]{1,0:T(8,128)}), f32[128,256]{1,0:T(8,128)}) %reduce-scatter.3.cloned.1.call-update) | async-done | bytes 131088 | tf_op jit(solution)/shard_map/reduce_scatter | solution.py:53
  162.5 0.0 copy-done.3
  162.5 0.0 copy-done.4
  162.5 1.6 convert_reduce_fusion
  164.2 5.5 collective-permute-start.1
  169.6 3.7 collective-permute-done.1
  173.3 0.7 pad_maximum_fusion.2
  174.0 0.0 all-gather.5.cloned.1.call-update
  174.0 0.0 reduce-scatter.5.cloned.1.call-start
  174.1 86.9 %all-gather.5.cloned.1.call-done = bf16[64,128,256]{2,1,0:T(8,128)(2,1)} async-done(((bf16[2,128,256]{2,1,0:T(8,128)(2,1)}), bf16[64,128,256]{2,1,0:T(8,128)(2,1)}) %all-gather.5.cloned.1.call-update) | async-done | bytes 4194320 | tf_op jit(solution)/shard_map/all_gather | solution.py:23
  260.9 8.2 %gather_fusion.1 = bf16[96,128,256]{2,1,0:T(8,128)(2,1)} fusion(bf16[64,128,256]{2,1,0:T(8,128)(2,1)} %all-gather.5.cloned.1.call-done, s32[1024]{0:T(1024)S(1)} %pad_clamp_fusion), kind=kCustom, calls=%fused_computation.1.clone | custom fusion | bytes 12583296 | tf_op jit(solution)/shard_map/jit(_take)/gather | solution.py:36
  269.1 0.0 copy-start.2
  269.1 0.0 copy-start.1
  269.1 5.2 fusion
  274.3 0.0 reduce-scatter.5.cloned.1.call-update
  274.3 0.0 all-reduce.3.cloned.1.call-start
  274.4 38.0 %reduce-scatter.5.cloned.1.call-done = f32[128,256]{1,0:T(8,128)} async-done(((f32[1024,256]{1,0:T(8,128)}), f32[128,256]{1,0:T(8,128)}) %reduce-scatter.5.cloned.1.call-update) | async-done | bytes 131088 | tf_op jit(solution)/shard_map/reduce_scatter | solution.py:60
  312.3 0.0 copy-done.2
  312.3 1.1 convolution_bitcast_fusion
  313.5 0.7 pad_maximum_fusion
  314.2 0.0 all-reduce.3.cloned.1.call-update
  314.2 0.0 all-reduce.5.cloned.1.call-start
  314.3 153.2 %all-reduce.3.cloned.1.call-done = f32[257,256]{1,0:T(8,128)} async-done(((f32[257,256]{1,0:T(8,128)}), f32[257,256]{1,0:T(8,128)}) %all-reduce.3.cloned.1.call-update) | async-done | bytes 263184 | tf_op jit(solution)/shard_map/psum | solution.py:69
  467.4 0.0 all-reduce.5.cloned.1.call-update
  467.5 0.0 copy-done.1
  467.5 1.7 convolution_convert_fusion
  469.2 111.6 %all-reduce.5.cloned.1.call-done = f32[257,256]{1,0:T(8,128)} async-done(((f32[257,256]{1,0:T(8,128)}), f32[257,256]{1,0:T(8,128)}) %all-reduce.5.cloned.1.call-update) | async-done | bytes 263184 | tf_op jit(solution)/shard_map/psum | solution.py:70
  580.8 1.3 slice.13
  582.1 1.7 slice.12
  (1 shorter events, 0.0 us)
Async XLA Ops:
  7.2 112.1 %copy-start = (bf16[1,8,1,12,128,128]{5,4,3,2,1,0:T(8,128)(2,1)S(1)}, bf16[1,8,1,12,128,128]{5,4,3,2,1,0:T(8,128)(2,1)}, u32[]{:S(2)}) copy-start(bf16[1,8,1,12,128,128]{5,4,3,2,1,0:T(8,128)(2,1)} %param.13) | copy-start | bytes 9437188
  7.2 103.9 %all-gather.3.cloned.1.call-start = ((), (), s32[]{:S(2)}) async-start(), calls=%async_computation.2 | async-start | bytes 4325376 | tf_op jit(solution)/shard_map/all_gather | solution.py:23
  8.5 10.0 %collective-permute-start = (bf16[128,256]{1,0:T(8,128)(2,1)S(1)}, bf16[128,256]{1,0:T(8,128)(2,1)S(1)}, u32[]{:S(2)}, u32[]{:S(2)}) collective-permute-start(bf16[128,256]{1,0:T(8,128)(2,1)S(1)} %convolution_convert_fusion.1), channel_id=1, source_target_pairs={{0,32},{32,0},{1,33},{33,1},{2,34},{34,2},{3,35},{35,3},{4,36},{36... | collective-permute-start | bytes 196616 | tf_op jit(solution)/shard_map/ppermute | solution.py:21
  19.2 143.4 %reduce-scatter.3.cloned.1.call-start = ((), (), s32[]{:S(2)}) async-start(), calls=%async_computation.3 | async-start | bytes 1179648 | tf_op jit(solution)/shard_map/reduce_scatter | solution.py:53
  119.3 43.2 %copy-start.3 = (bf16[128,256]{1,0:T(8,128)(2,1)S(1)}, bf16[128,256]{1,0:T(8,128)(2,1)}, u32[]{:S(2)}) copy-start(bf16[128,256]{1,0:T(8,128)(2,1)} %param.11) | copy-start | bytes 196612
  119.3 43.2 %copy-start.4 = (f32[256]{0:T(256)S(1)}, f32[256]{0:T(256)}, u32[]{:S(2)}) copy-start(f32[256]{0:T(256)} %param.10) | copy-start | bytes 3076
  124.5 136.4 %all-gather.5.cloned.1.call-start = ((), (), s32[]{:S(2)}) async-start(), calls=%async_computation.4 | async-start | bytes 4325376 | tf_op jit(solution)/shard_map/all_gather | solution.py:23
  164.2 9.1 %collective-permute-start.1 = (bf16[128,256]{1,0:T(8,128)(2,1)S(1)}, bf16[128,256]{1,0:T(8,128)(2,1)S(1)}, u32[]{:S(2)}, u32[]{:S(2)}) collective-permute-start(bf16[128,256]{1,0:T(8,128)(2,1)S(1)} %get-tuple-element.6), channel_id=1, source_target_pairs={{0,32},{32,0},{1,33},{33,1},{2,34},{34,2},{3,35},{35,3},{4,36},{36... | collective-permute-start | bytes 196616 | tf_op jit(solution)/shard_map/ppermute | solution.py:21
  174.0 138.3 %reduce-scatter.5.cloned.1.call-start = ((), (), s32[]{:S(2)}) async-start(), calls=%async_computation.5 | async-start | bytes 1179648 | tf_op jit(solution)/shard_map/reduce_scatter | solution.py:60
  269.1 43.2 %copy-start.2 = (bf16[128,256]{1,0:T(8,128)(2,1)S(1)}, bf16[128,256]{1,0:T(8,128)(2,1)}, u32[]{:S(2)}) copy-start(bf16[128,256]{1,0:T(8,128)(2,1)} %param.8) | copy-start | bytes 196612
  269.1 198.3 %copy-start.1 = (bf16[256,256]{1,0:T(8,128)(2,1)S(1)}, bf16[256,256]{1,0:T(8,128)(2,1)}, u32[]{:S(2)}) copy-start(bf16[256,256]{1,0:T(8,128)(2,1)} %param.9) | copy-start | bytes 393220
  274.3 193.1 %all-reduce.3.cloned.1.call-start = ((), (), s32[]{:S(2)}) async-start(), calls=%async_computation.6 | async-start | bytes 540672 | tf_op jit(solution)/shard_map/psum | solution.py:69
  314.2 266.6 %all-reduce.5.cloned.1.call-start = ((), (), s32[]{:S(2)}) async-start(), calls=%async_computation.7 | async-start | bytes 540672 | tf_op jit(solution)/shard_map/psum | solution.py:70
Sparse Core Ops, SparseCore 0:
  19.3 91.7 all-gather.2
  124.6 37.8 reduce-scatter.2
  174.1 86.7 all-gather.4
  274.5 37.8 reduce-scatter.4
  315.6 151.7 all-reduce.2
  469.6 111.1 all-reduce.4
where the time goes:
time: 591 us
  waiting for transfers between devices  524 us (89%)
  local copies, waits for them, and re-layouts  19.4 us (3%)
  matrix products  14.5 us (2%)
  between operations  14.2 us (2%)
  starting transfers between devices  14 us (2%)
    all_gather x2, waiting for transfers between devices, gather_team(): full = lax.all_gather(pair, PLANE, axis=0, tiled=True)  178 us
    psum x1, waiting for transfers between devices, local(): both = lax.psum(both, PLANE)  153 us
    psum x1, waiting for transfers between devices, local(): both = lax.psum(both, ('y_lo', 'y_hi', 'core'))  112 us
    reduce_scatter x1, waiting for transfers between devices, local(): lax.psum_scatter(partial_back, BLK_AXES, scatter_dimension=0, tiled=True)  38 us
    reduce_scatter x1, waiting for transfers between devices, local(): lax.psum_scatter(partial_rows, BLK_AXES, scatter_dimension=0, tiled=True)  38 us
    gather x2, local copies, waits for them, and re-layouts, collect(): picked = jnp.take(stacked, slots, axis=0)  16.4 us
    ppermute x2, starting transfers between devices, gather_team(): other = lax.ppermute(rows, 'y_hi', perm=[(0, 1), (1, 0)])  13.7 us
  transfers between devices with their start and end apart: 8, of which 8 were waited for; matrix products, arithmetic and copies ran while one was open for 0% of the time, Pallas kernels for 0%

commit v1 on v0

--- a/solution.py
+++ b/solution.py
@@ -66,7 +66,8 @@
     )
     local_bias = jnp.sum(pulled.astype(jnp.float32), axis=0)
     both = jnp.concatenate([local_weight, local_bias[None, :]], axis=0)
-    both = lax.psum(both, PLANE)
+    partial = lax.psum(both, "z")
+    both = lax.psum(partial, "x")
     both = lax.psum(both, ("y_lo", "y_hi", "core"))
     grad_weight = both[:-1]
     grad_bias = both[-1]

time: 591 us -> 570 us (0.964)
  waiting for transfers between devices: 524 us -> 503 us
    psum x1 -> x2, waiting for transfers between devices: 153 us -> 130 us  [the longest x1 75.7 us: local(): partial = lax.psum(both, 'z')]
  transfers between devices with their start and end apart: 8 -> 9, of which waited for: 8 -> 9; matrix products, arithmetic and copies ran while one was open for 0% -> 0% of each run, Pallas kernels for 0% -> 0%
where the time goes in v1:
time: 570 us; the launch traced here: 569 us
  waiting for transfers between devices  503 us (88%)
  local copies, waits for them, and re-layouts  19.4 us (3%)
  matrix products  14.5 us (3%)
  between operations  14.2 us (2%)
  starting transfers between devices  14 us (2%)
    all_gather x2, waiting for transfers between devices, gather_team(): full = lax.all_gather(pair, PLANE, axis=0, tiled=True)  178 us
    psum x1, waiting for transfers between devices, local(): both = lax.psum(both, ('y_lo', 'y_hi', 'core'))  113 us
    psum x1, waiting for transfers between devices, local(): partial = lax.psum(both, 'z')  75.7 us
    psum x1, waiting for transfers between devices, local(): both = lax.psum(partial, 'x')  54.8 us
    reduce_scatter x1, waiting for transfers between devices, local(): lax.psum_scatter(partial_back, BLK_AXES, scatter_dimension=0, tiled=True)  38 us
    reduce_scatter x1, waiting for transfers between devices, local(): lax.psum_scatter(partial_rows, BLK_AXES, scatter_dimension=0, tiled=True)  38 us
    gather x2, local copies, waits for them, and re-layouts, collect(): picked = jnp.take(stacked, slots, axis=0)  16.4 us
    ppermute x2, starting transfers between devices, gather_team(): other = lax.ppermute(rows, 'y_hi', perm=[(0, 1), (1, 0)])  13.7 us
  transfers between devices with their start and end apart: 9, of which 9 were waited for; matrix products, arithmetic and copies ran while one was open for 0% of the time, Pallas kernels for 0%

profile of v1, /device:TPU:1, one launch (start us, length us, event | category | flops | bytes accessed | tf_op | source)
XLA Modules:
  0.0 569.4 jit_solution(75321327353494652)
XLA Ops:
  7.2 0.0 copy-start
  7.2 0.0 all-gather.3.cloned.1.call-start
  7.2 1.2 convolution_convert_fusion.1
  8.5 8.3 %collective-permute-start = (bf16[128,256]{1,0:T(8,128)(2,1)S(1)}, bf16[128,256]{1,0:T(8,128)(2,1)S(1)}, u32[]{:S(2)}, u32[]{:S(2)}) collective-permute-start(bf16[128,256]{1,0:T(8,128)(2,1)S(1)} %convolution_convert_fusion.1), channel_id=1, source_target_pairs={{0,32},{32,0},{1,33},{33,1},{2,34},{34,2},{3,35},{35,3},{4,36},{36... | collective-permute-start | bytes 196616 | tf_op jit(solution)/shard_map/ppermute | solution.py:21
  16.8 1.7 collective-permute-done
  18.5 0.7 pad_maximum_fusion.1
  19.1 0.0 all-gather.3.cloned.1.call-update
  19.2 0.0 reduce-scatter.3.cloned.1.call-start
  19.2 0.7 compare_and_fusion
  19.9 0.1 reshape.42
  20.0 91.1 %all-gather.3.cloned.1.call-done = bf16[64,128,256]{2,1,0:T(8,128)(2,1)} async-done(((bf16[2,128,256]{2,1,0:T(8,128)(2,1)}), bf16[64,128,256]{2,1,0:T(8,128)(2,1)}) %all-gather.3.cloned.1.call-update) | async-done | bytes 4194320 | tf_op jit(solution)/shard_map/all_gather | solution.py:23
  111.1 8.2 %gather_fusion = bf16[96,128,256]{2,1,0:T(8,128)(2,1)} fusion(bf16[64,128,256]{2,1,0:T(8,128)(2,1)} %all-gather.3.cloned.1.call-done, s32[1024]{0:T(1024)S(1)} %pad_clamp_fusion), kind=kCustom, calls=%fused_computation.clone | custom fusion | bytes 12583296 | tf_op jit(solution)/shard_map/jit(_take)/gather | solution.py:36
  119.3 0.0 copy-done
  119.3 0.0 copy-start.3
  119.3 0.0 copy-start.4
  119.3 5.2 fusion.2
  124.5 0.0 reduce-scatter.3.cloned.1.call-update
  124.5 0.0 all-gather.5.cloned.1.call-start
  124.6 38.0 %reduce-scatter.3.cloned.1.call-done = f32[128,256]{1,0:T(8,128)} async-done(((f32[1024,256]{1,0:T(8,128)}), f32[128,256]{1,0:T(8,128)}) %reduce-scatter.3.cloned.1.call-update) | async-done | bytes 131088 | tf_op jit(solution)/shard_map/reduce_scatter | solution.py:53
  162.5 0.0 copy-done.3
  162.5 0.0 copy-done.4
  162.5 1.6 convert_reduce_fusion
  164.2 5.5 collective-permute-start.1
  169.6 3.7 collective-permute-done.1
  173.3 0.7 pad_maximum_fusion.2
  174.0 0.0 all-gather.5.cloned.1.call-update
  174.0 0.0 reduce-scatter.5.cloned.1.call-start
  174.1 86.9 %all-gather.5.cloned.1.call-done = bf16[64,128,256]{2,1,0:T(8,128)(2,1)} async-done(((bf16[2,128,256]{2,1,0:T(8,128)(2,1)}), bf16[64,128,256]{2,1,0:T(8,128)(2,1)}) %all-gather.5.cloned.1.call-update) | async-done | bytes 4194320 | tf_op jit(solution)/shard_map/all_gather | solution.py:23
  260.9 8.2 %gather_fusion.1 = bf16[96,128,256]{2,1,0:T(8,128)(2,1)} fusion(bf16[64,128,256]{2,1,0:T(8,128)(2,1)} %all-gather.5.cloned.1.call-done, s32[1024]{0:T(1024)S(1)} %pad_clamp_fusion), kind=kCustom, calls=%fused_computation.1.clone | custom fusion | bytes 12583296 | tf_op jit(solution)/shard_map/jit(_take)/gather | solution.py:36
  269.1 0.0 copy-start.2
  269.1 0.0 copy-start.1
  269.1 5.2 fusion
  274.3 0.0 reduce-scatter.5.cloned.1.call-update
  274.3 0.0 all-reduce.4.cloned.1.call-start
  274.4 38.0 %reduce-scatter.5.cloned.1.call-done = f32[128,256]{1,0:T(8,128)} async-done(((f32[1024,256]{1,0:T(8,128)}), f32[128,256]{1,0:T(8,128)}) %reduce-scatter.5.cloned.1.call-update) | async-done | bytes 131088 | tf_op jit(solution)/shard_map/reduce_scatter | solution.py:60
  312.3 0.0 copy-done.2
  312.3 1.1 convolution_bitcast_fusion
  313.5 0.7 pad_maximum_fusion
  314.2 0.0 all-reduce.4.cloned.1.call-update
  314.2 0.0 all-reduce.6.cloned.1.call-start
  314.3 75.7 %all-reduce.4.cloned.1.call-done = f32[257,256]{1,0:T(8,128)} async-done(((f32[257,256]{1,0:T(8,128)}), f32[257,256]{1,0:T(8,128)}) %all-reduce.4.cloned.1.call-update) | async-done | bytes 263184 | tf_op jit(solution)/shard_map/psum | solution.py:69
  389.9 0.0 all-reduce.6.cloned.1.call-update
  390.0 0.0 all-reduce.8.cloned.1.call-start
  390.0 54.8 %all-reduce.6.cloned.1.call-done = f32[257,256]{1,0:T(8,128)} async-done(((f32[257,256]{1,0:T(8,128)}), f32[257,256]{1,0:T(8,128)}) %all-reduce.6.cloned.1.call-update) | async-done | bytes 263184 | tf_op jit(solution)/shard_map/psum | solution.py:70
  444.8 0.0 all-reduce.8.cloned.1.call-update
  444.8 0.0 copy-done.1
  444.9 1.7 convolution_convert_fusion
  446.6 113.0 %all-reduce.8.cloned.1.call-done = f32[257,256]{1,0:T(8,128)} async-done(((f32[257,256]{1,0:T(8,128)}), f32[257,256]{1,0:T(8,128)}) %all-reduce.8.cloned.1.call-update) | async-done | bytes 263184 | tf_op jit(solution)/shard_map/psum | solution.py:71
  559.6 1.3 slice.13
  560.9 1.7 slice.12
  (1 shorter events, 0.0 us)
Async XLA Ops:
  7.2 112.1 %copy-start = (bf16[1,8,1,12,128,128]{5,4,3,2,1,0:T(8,128)(2,1)S(1)}, bf16[1,8,1,12,128,128]{5,4,3,2,1,0:T(8,128)(2,1)}, u32[]{:S(2)}) copy-start(bf16[1,8,1,12,128,128]{5,4,3,2,1,0:T(8,128)(2,1)} %param.13) | copy-start | bytes 9437188
  7.2 103.9 %all-gather.3.cloned.1.call-start = ((), (), s32[]{:S(2)}) async-start(), calls=%async_computation.2 | async-start | bytes 4325376 | tf_op jit(solution)/shard_map/all_gather | solution.py:23
  8.5 10.0 %collective-permute-start = (bf16[128,256]{1,0:T(8,128)(2,1)S(1)}, bf16[128,256]{1,0:T(8,128)(2,1)S(1)}, u32[]{:S(2)}, u32[]{:S(2)}) collective-permute-start(bf16[128,256]{1,0:T(8,128)(2,1)S(1)} %convolution_convert_fusion.1), channel_id=1, source_target_pairs={{0,32},{32,0},{1,33},{33,1},{2,34},{34,2},{3,35},{35,3},{4,36},{36... | collective-permute-start | bytes 196616 | tf_op jit(solution)/shard_map/ppermute | solution.py:21
  19.2 143.4 %reduce-scatter.3.cloned.1.call-start = ((), (), s32[]{:S(2)}) async-start(), calls=%async_computation.3 | async-start | bytes 1179648 | tf_op jit(solution)/shard_map/reduce_scatter | solution.py:53
  119.3 43.2 %copy-start.3 = (bf16[128,256]{1,0:T(8,128)(2,1)S(1)}, bf16[128,256]{1,0:T(8,128)(2,1)}, u32[]{:S(2)}) copy-start(bf16[128,256]{1,0:T(8,128)(2,1)} %param.11) | copy-start | bytes 196612
  119.3 43.2 %copy-start.4 = (f32[256]{0:T(256)S(1)}, f32[256]{0:T(256)}, u32[]{:S(2)}) copy-start(f32[256]{0:T(256)} %param.10) | copy-start | bytes 3076
  124.5 136.4 %all-gather.5.cloned.1.call-start = ((), (), s32[]{:S(2)}) async-start(), calls=%async_computation.4 | async-start | bytes 4325376 | tf_op jit(solution)/shard_map/all_gather | solution.py:23
  164.2 9.1 %collective-permute-start.1 = (bf16[128,256]{1,0:T(8,128)(2,1)S(1)}, bf16[128,256]{1,0:T(8,128)(2,1)S(1)}, u32[]{:S(2)}, u32[]{:S(2)}) collective-permute-start(bf16[128,256]{1,0:T(8,128)(2,1)S(1)} %get-tuple-element.6), channel_id=1, source_target_pairs={{0,32},{32,0},{1,33},{33,1},{2,34},{34,2},{3,35},{35,3},{4,36},{36... | collective-permute-start | bytes 196616 | tf_op jit(solution)/shard_map/ppermute | solution.py:21
  174.0 138.3 %reduce-scatter.5.cloned.1.call-start = ((), (), s32[]{:S(2)}) async-start(), calls=%async_computation.5 | async-start | bytes 1179648 | tf_op jit(solution)/shard_map/reduce_scatter | solution.py:60
  269.1 43.2 %copy-start.2 = (bf16[128,256]{1,0:T(8,128)(2,1)S(1)}, bf16[128,256]{1,0:T(8,128)(2,1)}, u32[]{:S(2)}) copy-start(bf16[128,256]{1,0:T(8,128)(2,1)} %param.8) | copy-start | bytes 196612
  269.1 175.7 %copy-start.1 = (bf16[256,256]{1,0:T(8,128)(2,1)S(1)}, bf16[256,256]{1,0:T(8,128)(2,1)}, u32[]{:S(2)}) copy-start(bf16[256,256]{1,0:T(8,128)(2,1)} %param.9) | copy-start | bytes 393220
  274.3 115.6 %all-reduce.4.cloned.1.call-start = ((), (), s32[]{:S(2)}) async-start(), calls=%async_computation.6 | async-start | bytes 540672 | tf_op jit(solution)/shard_map/psum | solution.py:69
  314.2 130.6 %all-reduce.6.cloned.1.call-start = ((), (), s32[]{:S(2)}) async-start(), calls=%async_computation.7 | async-start | bytes 540672 | tf_op jit(solution)/shard_map/psum | solution.py:70
  390.0 169.6 %all-reduce.8.cloned.1.call-start = ((), (), s32[]{:S(2)}) async-start(), calls=%async_computation.8 | async-start | bytes 540672 | tf_op jit(solution)/shard_map/psum | solution.py:71
Sparse Core Ops, SparseCore 0:
  19.3 91.7 all-gather.2
  124.6 37.8 reduce-scatter.2
  174.1 86.7 all-gather.4
  274.5 37.8 reduce-scatter.4
  314.5 75.3 all-reduce.3
  392.3 52.5 all-reduce.5
  447.3 112.2 all-reduce.7
